TPU v7x, 1024 devices: a whole 4x8x16 slice. The times are simulated.
1024 devices in a mesh: sens: 4 (over y_hi), par: 256 (over z, x, y_lo, core).
Axes of the slice: x: 4, y: 8 (y_hi: 4, y_lo: 2; y = y_hi * 2 + y_lo), z: 16, core: 2. Of those that a mesh axis runs over, the one named last changes fastest.
Arguments:
- probes: bfloat16 [2, 512, 8192], P(None, 'sens', 'par'), may hold values from -6 to 6
- green_blocks: bfloat16 [2, 262144, 512], P(None, 'par', 'sens'), may hold values from -0.25 to 0.25
- noise_table: float32 [64, 8], replicated, may hold values from 0.3 to 4
- station_class: int32 [512], P('sens'), may hold values from 0 to 7
- kappa_table: float32 [16], replicated, may hold values from 0.1 to 4
- coeff_index: int32 [4096], replicated, may hold values from 0 to 15
Outputs:
- hess_probes: float32 [2, 512, 8192], P(None, 'sens', 'par')
All inputs are finite; a program needn't handle non-finite values.
Results may differ from a plain program's by a relative error of at most 0.003.
Values may be sent and summed in bfloat16 or wider, within the bound.
A program may use at most 32 MiB of HBM per device.

v0:
```python
import jax
import jax.numpy as jnp
from jax import lax
from jax.sharding import PartitionSpec as P

SPLIT = 4
DIP = 32


def shortened(value):
    return jax.tree.map(lambda a: a.astype(jnp.bfloat16) if a.dtype == jnp.float32 else a, value)


def shifted(block, axis, distance):
    devices = range(lax.axis_size(axis))
    route = [(i - distance, i) for i in devices if i - distance in devices]
    return lax.ppermute(block, axis, route)


def swapped(value, axis, apart):
    return lax.ppermute(value, axis, [(i, i ^ 1 << apart) for i in range(lax.axis_size(axis))])


def neighbours(values, nfreq):
    left_rim = shifted(shortened(values[:, -1:]), "par", nfreq)
    right_rim = shifted(shortened(values[:, :1]), "par", -nfreq)
    along = jnp.concatenate([left_rim, values[:, :-1]], axis=1) + jnp.concatenate(
        [values[:, 1:], right_rim], axis=1
    )
    dipped = jnp.pad(values, ((0, 0), (0, 0), (1, 1), (0, 0)))
    return along + dipped[:, :, 2:] + dipped[:, :, :-2]


def sweeps(source, diagonal, nfreq):
    first_sweep = source / diagonal
    second_sweep = (source + neighbours(first_sweep, nfreq)) / diagonal
    return ((source + neighbours(second_sweep, nfreq)) / diagonal).astype(jnp.bfloat16)


def adjoint(green_part, probe_part):
    real_src = jnp.dot(green_part[0], probe_part[0], preferred_element_type=jnp.float32) + jnp.dot(
        green_part[1], probe_part[1], preferred_element_type=jnp.float32
    )
    imag_src = jnp.dot(green_part[0], probe_part[1], preferred_element_type=jnp.float32) - jnp.dot(
        green_part[1], probe_part[0], preferred_element_type=jnp.float32
    )
    return jnp.stack([real_src, imag_src])


def forward(green_part, slip_all):
    form = "cs,cr->sr"
    real_data = jnp.einsum(
        form, green_part[0], slip_all[0], preferred_element_type=jnp.float32
    ) - jnp.einsum(form, green_part[1], slip_all[1], preferred_element_type=jnp.float32)
    imag_data = jnp.einsum(
        form, green_part[0], slip_all[1], preferred_element_type=jnp.float32
    ) + jnp.einsum(form, green_part[1], slip_all[0], preferred_element_type=jnp.float32)
    return jnp.stack([real_data, imag_data])


def shards(probes, green_blocks, noise_table, station_class, kappa_table, coeff_index):
    cells_dev = green_blocks.shape[1]
    rows_dev = probes.shape[2]
    strike_dev = cells_dev // DIP
    nfreq = noise_table.shape[0]
    bit_count = SPLIT.bit_length() - 1
    bit_base = nfreq.bit_length() - 1
    highest = lax.Precision.HIGHEST
    par_index = lax.axis_index("par")
    freq_index = par_index % nfreq
    local_part = par_index // nfreq
    groups = noise_table.shape[1]
    station_hot = (station_class[:, None] == jnp.arange(groups, dtype=jnp.int32)[None, :]).astype(
        jnp.float32
    )
    variance = jnp.dot(station_hot, noise_table.T, precision=highest)
    weight = 1.0 / jnp.sqrt(variance)
    freq_hot = (jnp.arange(nfreq, dtype=jnp.int32) == freq_index).astype(jnp.float32)
    weight_col = jnp.dot(weight, freq_hot, precision=highest)
    joined = (weight_col[None, :, None] * probes.astype(jnp.float32)).astype(jnp.bfloat16)
    for bit_pos in range(bit_count):
        partner = swapped(joined, "par", bit_base + bit_pos)
        upper_side = par_index // 2 ** (bit_base + bit_pos) % 2 == 1
        joined = jnp.where(
            upper_side,
            jnp.concatenate([partner, joined], axis=2),
            jnp.concatenate([joined, partner], axis=2),
        )
    classes = kappa_table.shape[0]
    own_index = lax.dynamic_slice_in_dim(coeff_index, local_part * cells_dev, cells_dev, 0)
    class_hot = (own_index[:, None] == jnp.arange(classes, dtype=jnp.int32)[None, :]).astype(
        jnp.float32
    )
    kappa_cell = jnp.dot(class_hot, kappa_table, precision=highest)
    diagonal = (4.0 + kappa_cell).reshape(1, strike_dev, DIP, 1)
    partial_src = adjoint(green_blocks, joined)
    row_share = lax.psum_scatter(partial_src, "sens", scatter_dimension=2, tiled=True)
    share_rows = row_share.shape[2]
    slip_tile = sweeps(row_share.reshape(2, strike_dev, DIP, share_rows), diagonal, nfreq)
    slip_all = lax.all_gather(
        slip_tile.reshape(2, cells_dev, share_rows), "sens", axis=2, tiled=True
    )
    partial_data = forward(green_blocks, slip_all)
    totals = partial_data
    for bit_pos in range(bit_count):
        totals = totals + swapped(totals, "par", bit_base + bit_pos)
    own_rows = lax.dynamic_slice_in_dim(totals, local_part * rows_dev, rows_dev, 2)
    return weight_col[None, :, None] * own_rows


def solution(mesh):
    in_specs = (P(None, "sens", "par"), P(None, "par", "sens"), P(), P("sens"), P(), P())
    out_specs = P(None, "sens", "par")
    return jax.shard_map(shards, mesh=mesh, in_specs=in_specs, out_specs=out_specs, check_vma=False)
```

profile of v0, /device:TPU:8, one launch (start us, length us, event | category | flops | bytes accessed | tf_op | source)
XLA Modules:
  0.0 184.1 jit_solution(5339254141309329323)
XLA Ops:
  6.5 0.0 copy-start
  6.5 0.0 reduce-scatter.2.cloned.1.call-start
  6.5 0.0 copy-start.3
  6.5 0.7 copy-done
  7.2 0.0 copy-done.3
  7.2 0.2 convolution_rsqrt_fusion
  7.5 0.0 copy-start.2
  7.5 0.1 convolution_bitcast_fusion
  7.6 0.6 copy-done.2
  8.2 10.9 %collective-permute-start = (bf16[2,128,32]{1,2,0:T(8,128)(2,1)S(1)}, bf16[2,128,32]{1,2,0:T(8,128)(2,1)S(1)}, u32[]{:S(2)}, u32[]{:S(2)}) collective-permute-start(bf16[2,128,32]{1,2,0:T(8,128)(2,1)S(1)} %multiply_convert_fusion), channel_id=1, source_target_pairs={{0,64},{1,65},{2,66},{3,67},{4,68},{5,69},{6,70},{7,71},{8,72},{9,... | collective-permute-start | bytes 49160 | tf_op jit(solution)/shard_map/ppermute | solution.py:21
  19.1 0.0 copy-start.1
  19.1 1.7 collective-permute-done
  20.8 16.3 %collective-permute-start.1 = (bf16[2,128,64]{1,2,0:T(8,128)(2,1)S(1)}, bf16[2,128,64]{1,2,0:T(8,128)(2,1)S(1)}, u32[]{:S(2)}, u32[]{:S(2)}) collective-permute-start(bf16[2,128,64]{1,2,0:T(8,128)(2,1)S(1)} %maximum_select_fusion.1), channel_id=1, source_target_pairs={{0,128},{1,129},{2,130},{3,131},{4,132},{5,133},{6,134},{7,135},{8... | collective-permute-start | bytes 98312 | tf_op jit(solution)/shard_map/ppermute | solution.py:21
  37.1 1.9 %collective-permute-done.1 = bf16[2,128,64]{1,2,0:T(8,128)(2,1)S(1)} collective-permute-done((bf16[2,128,64]{1,2,0:T(8,128)(2,1)S(1)}, bf16[2,128,64]{1,2,0:T(8,128)(2,1)S(1)}, u32[]{:S(2)}, u32[]{:S(2)}) %collective-permute-start.1) | collective-permute-done | bytes 32800 | tf_op jit(solution)/shard_map/ppermute | solution.py:21
  39.0 1.2 fusion.22
  40.2 0.0 copy-done.1
  40.2 0.2 fusion.24
  40.5 0.2 fusion
  40.7 0.2 fusion.1
  40.9 1.1 pad_maximum_fusion
  42.0 0.0 reduce-scatter.2.cloned.1.call-update
  42.1 0.0 dynamic-slice-start
  42.1 0.0 copy-start.4
  42.1 0.7 dynamic-slice-done
  42.8 0.0 copy-done.4
  42.8 0.4 fusion.13
  43.2 0.1 div.46
  43.3 40.4 %reduce-scatter.2.cloned.1.call-done = f32[2,1024,32]{1,2,0:T(8,128)} async-done(((f32[2,1024,128]{1,2,0:T(8,128)}), f32[2,1024,32]{1,2,0:T(8,128)}) %reduce-scatter.2.cloned.1.call-update) | async-done | bytes 262160 | tf_op jit(solution)/shard_map/reduce_scatter | solution.py:97
  83.7 1.3 reshape.11
  85.0 0.2 fusion.45
  85.2 0.1 fusion.49
  85.3 8.2 %collective-permute-start.2 = (bf16[2,1,32,32]{2,1,3,0:T(2,128)(2,1)S(1)}, bf16[2,1,32,32]{2,1,3,0:T(2,128)(2,1)S(1)}, u32[]{:S(2)}, u32[]{:S(2)}) collective-permute-start(bf16[2,1,32,32]{2,1,3,0:T(2,128)(2,1)S(1)} %get-tuple-element.15), channel_id=1, source_target_pairs={{0,64},{1,65},{2,66},{3,67},{4,68},{5,69},{6,70},{7,71},{8,72},{9,... | collective-permute-start | bytes 12296 | tf_op jit(solution)/shard_map/ppermute | solution.py:17
  93.5 1.3 collective-permute-start.3
  94.8 0.2 fusion.47
  95.0 0.0 collective-permute-done.2
  95.1 8.3 %collective-permute-done.3 = bf16[2,1,32,32]{2,1,3,0:T(2,128)(2,1)S(1)} collective-permute-done((bf16[2,1,32,32]{2,1,3,0:T(2,128)(2,1)S(1)}, bf16[2,1,32,32]{2,1,3,0:T(2,128)(2,1)S(1)}, u32[]{:S(2)}, u32[]{:S(2)}) %collective-permute-start.3) | collective-permute-done | bytes 4128 | tf_op jit(solution)/shard_map/ppermute | solution.py:17
  103.4 0.7 fusion.43
  104.1 0.1 fusion.48
  104.2 9.2 %collective-permute-start.4 = (bf16[2,1,32,32]{2,1,3,0:T(2,128)(2,1)S(1)}, bf16[2,1,32,32]{2,1,3,0:T(2,128)(2,1)S(1)}, u32[]{:S(2)}, u32[]{:S(2)}) collective-permute-start(bf16[2,1,32,32]{2,1,3,0:T(2,128)(2,1)S(1)} %get-tuple-element.13), channel_id=1, source_target_pairs={{0,64},{1,65},{2,66},{3,67},{4,68},{5,69},{6,70},{7,71},{8,72},{9,... | collective-permute-start | bytes 12296 | tf_op jit(solution)/shard_map/ppermute | solution.py:17
  113.4 1.3 collective-permute-start.5
  114.7 0.2 fusion.46
  114.9 0.0 collective-permute-done.4
  115.0 8.6 %collective-permute-done.5 = bf16[2,1,32,32]{2,1,3,0:T(2,128)(2,1)S(1)} collective-permute-done((bf16[2,1,32,32]{2,1,3,0:T(2,128)(2,1)S(1)}, bf16[2,1,32,32]{2,1,3,0:T(2,128)(2,1)S(1)}, u32[]{:S(2)}, u32[]{:S(2)}) %collective-permute-start.5) | collective-permute-done | bytes 4128 | tf_op jit(solution)/shard_map/ppermute | solution.py:17
  123.6 0.7 fusion.12
  124.3 0.5 reshape.12
  124.8 17.0 %all_gather.3 = bf16[2,1024,128]{1,2,0:T(8,128)(2,1)S(1)} all-gather(bf16[2,1024,32]{1,2,0:T(8,128)(2,1)S(1)} %reshape.12), channel_id=1, replica_groups=mesh['sens'=4,'par'=256] {'sens'}, dimensions={2}, use_global_device_ids=true | all-gather | bytes 655360 | tf_op jit(solution)/shard_map/all_gather | solution.py:100
  141.9 0.2 fusion.18
  142.1 0.2 fusion.20
  142.3 0.2 fusion.2
  142.5 0.2 fusion.3
  142.8 2.0 %collective-permute-start.6 = (f32[2,128,128]{1,2,0:T(8,128)S(1)}, f32[2,128,128]{1,2,0:T(8,128)S(1)}, u32[]{:S(2)}, u32[]{:S(2)}) collective-permute-start(f32[2,128,128]{1,2,0:T(8,128)S(1)} %pad_maximum_fusion.1), channel_id=1, source_target_pairs={{0,64},{1,65},{2,66},{3,67},{4,68},{5,69},{6,70},{7,71},{8,72},{9,... | collective-permute-start | bytes 393224 | tf_op jit(solution)/shard_map/ppermute | solution.py:21
  144.7 16.3 %collective-permute-done.6 = f32[2,128,128]{1,2,0:T(8,128)S(1)} collective-permute-done((f32[2,128,128]{1,2,0:T(8,128)S(1)}, f32[2,128,128]{1,2,0:T(8,128)S(1)}, u32[]{:S(2)}, u32[]{:S(2)}) %collective-permute-start.6) | collective-permute-done | bytes 131104 | tf_op jit(solution)/shard_map/ppermute | solution.py:21
  161.1 1.9 %collective-permute-start.7 = (f32[2,128,128]{1,2,0:T(8,128)S(1)}, f32[2,128,128]{1,2,0:T(8,128)S(1)}, u32[]{:S(2)}, u32[]{:S(2)}) collective-permute-start(f32[2,128,128]{1,2,0:T(8,128)S(1)} %fusion.42), channel_id=1, source_target_pairs={{0,128},{1,129},{2,130},{3,131},{4,132},{5,133},{6,134},{7,135},{8... | collective-permute-start | bytes 393224 | tf_op jit(solution)/shard_map/ppermute | solution.py:21
  163.0 13.6 %collective-permute-done.7 = f32[2,128,128]{1,2,0:T(8,128)S(1)} collective-permute-done((f32[2,128,128]{1,2,0:T(8,128)S(1)}, f32[2,128,128]{1,2,0:T(8,128)S(1)}, u32[]{:S(2)}, u32[]{:S(2)}) %collective-permute-start.7) | collective-permute-done | bytes 131104 | tf_op jit(solution)/shard_map/ppermute | solution.py:21
  176.7 0.6 fusion.35
  (10 shorter events, 0.2 us)
Async XLA Ops:
  6.5 0.7 copy-start
  6.5 77.2 %reduce-scatter.2.cloned.1.call-start = ((), (), s32[]{:S(2)}) async-start(), calls=%async_computation.1 | async-start | bytes 1310720 | tf_op jit(solution)/shard_map/reduce_scatter | solution.py:97
  6.5 0.7 copy-start.3
  7.5 0.7 copy-start.2
  8.2 12.6 %collective-permute-start = (bf16[2,128,32]{1,2,0:T(8,128)(2,1)S(1)}, bf16[2,128,32]{1,2,0:T(8,128)(2,1)S(1)}, u32[]{:S(2)}, u32[]{:S(2)}) collective-permute-start(bf16[2,128,32]{1,2,0:T(8,128)(2,1)S(1)} %multiply_convert_fusion), channel_id=1, source_target_pairs={{0,64},{1,65},{2,66},{3,67},{4,68},{5,69},{6,70},{7,71},{8,72},{9,... | collective-permute-start | bytes 49160 | tf_op jit(solution)/shard_map/ppermute | solution.py:21
  19.1 21.1 %copy-start.1 = (bf16[2,1024,128]{2,1,0:T(8,128)(2,1)S(1)}, bf16[2,1024,128]{2,1,0:T(8,128)(2,1)}, u32[]{:S(2)}) copy-start(bf16[2,1024,128]{2,1,0:T(8,128)(2,1)} %param.7) | copy-start | bytes 1572868
  20.8 18.2 %collective-permute-start.1 = (bf16[2,128,64]{1,2,0:T(8,128)(2,1)S(1)}, bf16[2,128,64]{1,2,0:T(8,128)(2,1)S(1)}, u32[]{:S(2)}, u32[]{:S(2)}) collective-permute-start(bf16[2,128,64]{1,2,0:T(8,128)(2,1)S(1)} %maximum_select_fusion.1), channel_id=1, source_target_pairs={{0,128},{1,129},{2,130},{3,131},{4,132},{5,133},{6,134},{7,135},{8... | collective-permute-start | bytes 98312 | tf_op jit(solution)/shard_map/ppermute | solution.py:21
  42.1 0.7 dynamic-slice-start
  42.1 0.7 copy-start.4
  85.3 9.8 %collective-permute-start.2 = (bf16[2,1,32,32]{2,1,3,0:T(2,128)(2,1)S(1)}, bf16[2,1,32,32]{2,1,3,0:T(2,128)(2,1)S(1)}, u32[]{:S(2)}, u32[]{:S(2)}) collective-permute-start(bf16[2,1,32,32]{2,1,3,0:T(2,128)(2,1)S(1)} %get-tuple-element.15), channel_id=1, source_target_pairs={{0,64},{1,65},{2,66},{3,67},{4,68},{5,69},{6,70},{7,71},{8,72},{9,... | collective-permute-start | bytes 12296 | tf_op jit(solution)/shard_map/ppermute | solution.py:17
  93.5 9.9 %collective-permute-start.3 = (bf16[2,1,32,32]{2,1,3,0:T(2,128)(2,1)S(1)}, bf16[2,1,32,32]{2,1,3,0:T(2,128)(2,1)S(1)}, u32[]{:S(2)}, u32[]{:S(2)}) collective-permute-start(bf16[2,1,32,32]{2,1,3,0:T(2,128)(2,1)S(1)} %get-tuple-element.16), channel_id=1, source_target_pairs={{64,0},{65,1},{66,2},{67,3},{68,4},{69,5},{70,6},{71,7},{72,8},{73... | collective-permute-start | bytes 12296 | tf_op jit(solution)/shard_map/ppermute | solution.py:17
  104.2 10.8 %collective-permute-start.4 = (bf16[2,1,32,32]{2,1,3,0:T(2,128)(2,1)S(1)}, bf16[2,1,32,32]{2,1,3,0:T(2,128)(2,1)S(1)}, u32[]{:S(2)}, u32[]{:S(2)}) collective-permute-start(bf16[2,1,32,32]{2,1,3,0:T(2,128)(2,1)S(1)} %get-tuple-element.13), channel_id=1, source_target_pairs={{0,64},{1,65},{2,66},{3,67},{4,68},{5,69},{6,70},{7,71},{8,72},{9,... | collective-permute-start | bytes 12296 | tf_op jit(solution)/shard_map/ppermute | solution.py:17
  113.4 10.2 %collective-permute-start.5 = (bf16[2,1,32,32]{2,1,3,0:T(2,128)(2,1)S(1)}, bf16[2,1,32,32]{2,1,3,0:T(2,128)(2,1)S(1)}, u32[]{:S(2)}, u32[]{:S(2)}) collective-permute-start(bf16[2,1,32,32]{2,1,3,0:T(2,128)(2,1)S(1)} %get-tuple-element.14), channel_id=1, source_target_pairs={{64,0},{65,1},{66,2},{67,3},{68,4},{69,5},{70,6},{71,7},{72,8},{73... | collective-permute-start | bytes 12296 | tf_op jit(solution)/shard_map/ppermute | solution.py:17
  142.8 18.3 %collective-permute-start.6 = (f32[2,128,128]{1,2,0:T(8,128)S(1)}, f32[2,128,128]{1,2,0:T(8,128)S(1)}, u32[]{:S(2)}, u32[]{:S(2)}) collective-permute-start(f32[2,128,128]{1,2,0:T(8,128)S(1)} %pad_maximum_fusion.1), channel_id=1, source_target_pairs={{0,64},{1,65},{2,66},{3,67},{4,68},{5,69},{6,70},{7,71},{8,72},{9,... | collective-permute-start | bytes 393224 | tf_op jit(solution)/shard_map/ppermute | solution.py:21
  161.1 15.6 %collective-permute-start.7 = (f32[2,128,128]{1,2,0:T(8,128)S(1)}, f32[2,128,128]{1,2,0:T(8,128)S(1)}, u32[]{:S(2)}, u32[]{:S(2)}) collective-permute-start(f32[2,128,128]{1,2,0:T(8,128)S(1)} %fusion.42), channel_id=1, source_target_pairs={{0,128},{1,129},{2,130},{3,131},{4,132},{5,133},{6,134},{7,135},{8... | collective-permute-start | bytes 393224 | tf_op jit(solution)/shard_map/ppermute | solution.py:21
Sparse Core Ops, SparseCore 0:
  42.2 41.4 reduce-scatter.1
where the time goes:
time: 185 us; the launch traced here: 184 us
  waiting for transfers between devices  90.9 us (49%)
  starting transfers between devices  51 us (28%)
  blocking collectives  17 us (9%)
  between operations  13.7 us (7%)
  local copies, waits for them, and re-layouts  4.42 us (2%)
  other arithmetic  3.57 us (2%)
  matrix products  3.54 us (2%)
    reduce_scatter x1, waiting for transfers between devices, shards(): lax.psum_scatter(partial_src, 'sens', scatter_dimension=2, tiled=True)  40.4 us
    ppermute x4, waiting for transfers between devices, swapped(): lax.ppermute(value, axis, [(i, i ^ 1 << apart) for i in range(lax.axis_si...  33.5 us
    ppermute x4, starting transfers between devices, swapped(): lax.ppermute(value, axis, [(i, i ^ 1 << apart) for i in range(lax.axis_si...  31.1 us
    ppermute x4, starting transfers between devices, shifted(): return lax.ppermute(block, axis, route)  19.9 us
    all_gather x1, blocking collectives, shards(): lax.all_gather(slip_tile.reshape(2, cells_dev, share_rows), 'sens', axis=...  17 us
    ppermute x4, waiting for transfers between devices, shifted(): return lax.ppermute(block, axis, route)  16.9 us
  transfers between devices with their start and end apart: 9, of which 7 were waited for; matrix products, arithmetic and copies ran while one was open for 1% of the time, Pallas kernels for 0%

commit v1 on v0

v1 whole, which is shorter than its diff:
```python
import functools

import jax
import jax.numpy as jnp
from jax import lax
from jax.experimental import pallas as pl
from jax.experimental.pallas import tpu as pltpu
from jax.sharding import PartitionSpec as P

SPLIT = 4
SENS = 4
DIP = 32
MESH = pl.DeviceIdType.MESH
NT = (((1,), (1,)), ((), ()))


def kernel(
    nfreq, probes, noise, station, kappa, coeff, green, out,
    gbuf, zbuf, hsend, hrecv, ysend, yrecv, zsend, zrecv,
    own_sem, gs, gr, zys, zyr, zzs, zzr, hs, hr, ys, yr, zs, zr,
):
    sens = lax.axis_index("sens")
    par = lax.axis_index("par")
    part = par // nfreq
    freq = par % nfreq

    def sens_peer(k):
        return {"sens": (sens + k) % SENS, "par": par}

    def part_peer(j):
        return {"sens": sens, "par": (part + j) % SPLIT * nfreq + freq}

    def block_of(s):
        return s + part % 2 * (SENS - 1 - 2 * s)

    def send(src, dst, ssem, rsem, device):
        copy = pltpu.make_async_remote_copy(
            src_ref=src, dst_ref=dst, send_sem=ssem, recv_sem=rsem,
            device_id=device, device_id_type=MESH,
        )
        copy.start()
        return copy

    barrier = pltpu.get_barrier_semaphore()
    for k in range(1, SENS):
        pl.semaphore_signal(barrier, inc=1, device_id=sens_peer(k), device_id_type=MESH)
    for j in range(1, SPLIT):
        pl.semaphore_signal(barrier, inc=1, device_id=part_peer(j), device_id_type=MESH)

    cells = gbuf.shape[2]
    block = block_of(sens)
    own = pltpu.make_async_copy(
        green.at[:, pl.ds(pl.multiple_of(block * cells, cells), cells), :], gbuf.at[0], own_sem
    )
    own.start()

    lane = lax.broadcasted_iota(jnp.int32, noise.shape, 1)
    column = jnp.sum(jnp.where(lane == freq, noise[...], 0.0), axis=1, keepdims=True)
    group = lax.broadcasted_iota(jnp.int32, (noise.shape[0], station.shape[1]), 0)
    variance = jnp.sum(jnp.where(group == station[...], column, 0.0), axis=0, keepdims=True)
    weight = 1.0 / jnp.sqrt(variance)
    for c in range(2):
        zbuf[part, 0, c] = (weight * probes[c].astype(jnp.float32)).astype(jnp.bfloat16)

    pl.semaphore_wait(barrier, SENS - 1 + SPLIT - 1)

    zy = [
        send(zbuf.at[part, 0], zbuf.at[part, k], zys.at[k - 1], zyr.at[k - 1], sens_peer(k))
        for k in range(1, SENS)
    ]
    g = []
    for k in (1, 3, 2):
        theirs = block_of((sens + k) % SENS)
        rows = pl.ds(pl.multiple_of(theirs * cells, cells), cells)
        g.append(send(green.at[:, rows, :], gbuf.at[k], gs.at[k - 1], gr.at[k - 1], sens_peer(k)))

    place = part * SENS + block
    rows_all = coeff.shape[0]

    def inverse(row, keep):
        index = coeff[pl.ds((row + rows_all) % rows_all, 1), :]
        value = jnp.zeros(index.shape, jnp.float32)
        for n in range(kappa.shape[0]):
            value = jnp.where(index == n, kappa[n], value)
        value = jnp.where(keep, 1.0 / (4.0 + value), 0.0)
        return jnp.broadcast_to(value, (128, 128)).T

    first = place == 0
    last = place == SPLIT * SENS - 1
    before = inverse(2 * place - 1, jnp.logical_not(first))
    after = inverse(2 * place + 2, jnp.logical_not(last))
    inv = jnp.concatenate(
        [before[64:], inverse(2 * place, True), inverse(2 * place + 1, True), after[:64]], axis=0
    )
    inv = inv.reshape(12, DIP, 128)
    inv = jnp.concatenate([inv, inv], axis=2)

    for copy in zy:
        copy.wait()
    zz = [
        send(zbuf.at[part], zbuf.at[part], zzs.at[j - 1], zzr.at[j - 1], part_peer(j))
        for j in range(1, SPLIT)
    ]
    own.wait()
    for copy in zz:
        copy.wait()
    for copy in g:
        copy.wait()

    src = jnp.zeros((cells, 256), jnp.float32)
    for k in range(SENS):
        a = jnp.concatenate([gbuf[k, 0], gbuf[k, 1]], axis=1)
        z_re = zbuf[:, k, 0].reshape(128, 128)
        z_im = zbuf[:, k, 1].reshape(128, 128)
        b = jnp.concatenate(
            [jnp.concatenate([z_re, z_im], axis=1), jnp.concatenate([z_im, -z_re], axis=1)], axis=0
        )
        src += lax.dot_general(a, b, NT, preferred_element_type=jnp.float32)

    hsend[0] = src[:64].astype(jnp.bfloat16)
    hsend[1] = src[cells - 64 :].astype(jnp.bfloat16)

    def device_of(b):
        p = b // SENS
        r = b % SENS
        return {"sens": r + p % 2 * (SENS - 1 - 2 * r), "par": p * nfreq + freq}

    def rim(side, b):
        return pltpu.make_async_remote_copy(
            src_ref=hsend.at[side], dst_ref=hrecv.at[1 - side], send_sem=hs.at[side],
            recv_sem=hr.at[1 - side], device_id=device_of(b), device_id_type=MESH,
        )

    total = SPLIT * SENS

    @pl.when(place > 0)
    def _():
        rim(0, (place + total - 1) % total).start()

    @pl.when(place < total - 1)
    def _():
        rim(1, (place + 1) % total).start()

    @pl.when(place == 0)
    def _():
        hrecv[0] = jnp.zeros(hrecv.shape[1:], hrecv.dtype)

    @pl.when(place == total - 1)
    def _():
        hrecv[1] = jnp.zeros(hrecv.shape[1:], hrecv.dtype)

    @pl.when(place > 0)
    def _():
        copy = rim(0, (place + total - 1) % total)
        copy.wait_send()
        pltpu.make_async_remote_copy(
            src_ref=hsend.at[1], dst_ref=hrecv.at[0], send_sem=hs.at[1],
            recv_sem=hr.at[0], device_id=device_of((place + total - 1) % total), device_id_type=MESH,
        ).wait_recv()

    @pl.when(place < total - 1)
    def _():
        copy = rim(1, (place + 1) % total)
        copy.wait_send()
        pltpu.make_async_remote_copy(
            src_ref=hsend.at[0], dst_ref=hrecv.at[1], send_sem=hs.at[0],
            recv_sem=hr.at[1], device_id=device_of((place + 1) % total), device_id_type=MESH,
        ).wait_recv()

    full = jnp.concatenate(
        [hrecv[0].astype(jnp.float32), src, hrecv[1].astype(jnp.float32)], axis=0
    ).reshape(12, DIP, 256)

    def dips(u):
        zero = jnp.zeros((u.shape[0], 1, u.shape[2]), u.dtype)
        return jnp.concatenate([u[:, 1:], zero], axis=1) + jnp.concatenate([zero, u[:, :-1]], axis=1)

    u1 = full * inv
    u2 = (full[1:11] + u1[:10] + u1[2:] + dips(u1[1:11])) * inv[1:11]
    slip = (full[2:10] + u2[:8] + u2[2:] + dips(u2[1:9])) * inv[2:10]
    slip_t = slip.reshape(cells, 256).astype(jnp.bfloat16).T

    def data_of(k):
        b = jnp.concatenate([gbuf[k, 0], gbuf[k, 1]], axis=1)
        both = jnp.dot(slip_t, b, preferred_element_type=jnp.float32)
        return both[:128, :128] - both[128:, 128:], both[128:, :128] + both[:128, 128:]

    y = []
    for k in (2, 1, 3):
        re, im = data_of(k)
        ysend[k - 1, 0] = re
        ysend[k - 1, 1] = im
        y.append(
            send(ysend.at[k - 1], yrecv.at[k - 1], ys.at[k - 1], yr.at[k - 1], sens_peer(SENS - k))
        )
    re, im = data_of(0)
    for copy in y:
        copy.wait()
    total_data = []
    for c, part_sum in ((0, re), (1, im)):
        total_data.append(part_sum + yrecv[0, c] + yrecv[1, c] + yrecv[2, c])
    zc = []
    for p in range(SPLIT):
        for c in range(2):
            zsend[p, c] = total_data[c][p * 32 : (p + 1) * 32]
    for j in (2, 1, 3):
        zc.append(
            send(zsend.at[(part + SPLIT - j) % SPLIT], zrecv.at[j - 1], zs.at[j - 1], zr.at[j - 1], part_peer(SPLIT - j))
        )
    for copy in zc:
        copy.wait()
    for c in range(2):
        out[c] = weight * (zsend[part, c] + zrecv[0, c] + zrecv[1, c] + zrecv[2, c])


def shards(probes, green_blocks, noise_table, station_class, kappa_table, coeff_index):
    nfreq = noise_table.shape[0]
    bf16, f32 = jnp.bfloat16, jnp.float32
    dma = pltpu.SemaphoreType.DMA
    vmem = pl.BlockSpec(memory_space=pltpu.VMEM)
    result = pl.pallas_call(
        functools.partial(kernel, nfreq),
        out_shape=jax.ShapeDtypeStruct((2, 32, 128), f32),
        in_specs=[
            vmem, vmem, vmem, pl.BlockSpec(memory_space=pltpu.SMEM), vmem,
            pl.BlockSpec(memory_space=pl.ANY),
        ],
        out_specs=vmem,
        scratch_shapes=[
            pltpu.VMEM((4, 2, 256, 128), bf16),
            pltpu.VMEM((4, 4, 2, 32, 128), bf16),
            pltpu.VMEM((2, 64, 256), bf16),
            pltpu.VMEM((2, 64, 256), bf16),
            pltpu.VMEM((3, 2, 128, 128), f32),
            pltpu.VMEM((3, 2, 128, 128), f32),
            pltpu.VMEM((4, 2, 32, 128), f32),
            pltpu.VMEM((3, 2, 32, 128), f32),
            dma, dma((3,)), dma((3,)), dma((3,)), dma((3,)), dma((3,)), dma((3,)),
            dma((2,)), dma((2,)), dma((3,)), dma((3,)), dma((3,)), dma((3,)),
        ],
        compiler_params=pltpu.CompilerParams(collective_id=0, has_side_effects=True),
    )(
        probes.transpose(0, 2, 1), noise_table.T, station_class.reshape(1, -1), kappa_table,
        coeff_index.reshape(-1, 128), green_blocks,
    )
    return result.transpose(0, 2, 1)


def solution(mesh):
    in_specs = (P(None, "sens", "par"), P(None, "par", "sens"), P(), P("sens"), P(), P())
    out_specs = P(None, "sens", "par")
    return jax.shard_map(shards, mesh=mesh, in_specs=in_specs, out_specs=out_specs, check_vma=False)
```

time: 185 us -> 68.3 us (0.37)
  the two profiles are of different devices: /device:TPU:8 before, /device:TPU:128 now
where the time goes in v1:
time: 68.3 us; the launch traced here: 68 us
  Pallas kernels  66.6 us (98%)
  local copies, waits for them, and re-layouts  1.38 us (2%)
    pallas_call x1, Pallas kernels, shards(): pl.pallas_call(functools.partial(kernel, nfreq), out_shape=jax.ShapeDtype...  66.6 us
    unnamed x1, local copies, waits for them, and re-layouts  1.38 us

profile of v1, /device:TPU:128, one launch (start us, length us, event | category | flops | bytes accessed | tf_op | source)
XLA Modules:
  0.0 68.0 jit_solution(14146575742540447079)
XLA Ops:
  0.0 66.6 %shard_map.64 = f32[2,32,128]{2,1,0:T(8,128)} custom-call(bf16[2,32,128]{2,1,0:T(8,128)(2,1)} %bitcast.6, f32[8,64]{1,0:T(8,128)} %bitcast.8, s32[1,128]{1,0:T(1,128)} %bitcast.9, f32[16]{0:T(128)} %kappa.1, s32[32,128]{1,0:T(8,128)} %bitcast.7, bf16[2,1024,128]{2,1,0:T(8,128)(2,1)} %green.1), custom_call_target="tpu_custom_call" | custom-call | tf_op jit(solution)/shard_map/pallas_call | solution.py:221
  66.6 1.4 %copy.8 = f32[2,128,32]{1,2,0:T(8,128)} copy(f32[2,128,32]{1,2,0:T(8,128)} %bitcast.5) | data formatting | bytes 65536

commit v2 on v1

--- a/solution.py
+++ b/solution.py
@@ -16,7 +16,7 @@
 
 def kernel(
     nfreq, probes, noise, station, kappa, coeff, green, out,
-    gbuf, zbuf, hsend, hrecv, ysend, yrecv, zsend, zrecv,
+    gbuf, zbuf, hsend, hrecv, ysend, yrecv, tsum, zsend, zrecv,
     own_sem, gs, gr, zys, zyr, zzs, zzr, hs, hr, ys, yr, zs, zr,
 ):
     sens = lax.axis_index("sens")
@@ -188,8 +188,8 @@
     y = []
     for k in (2, 1, 3):
         re, im = data_of(k)
-        ysend[k - 1, 0] = re
-        ysend[k - 1, 1] = im
+        ysend[k - 1, 0] = re.astype(ysend.dtype)
+        ysend[k - 1, 1] = im.astype(ysend.dtype)
         y.append(
             send(ysend.at[k - 1], yrecv.at[k - 1], ys.at[k - 1], yr.at[k - 1], sens_peer(SENS - k))
         )
@@ -198,11 +198,12 @@
         copy.wait()
     total_data = []
     for c, part_sum in ((0, re), (1, im)):
-        total_data.append(part_sum + yrecv[0, c] + yrecv[1, c] + yrecv[2, c])
+        total_data.append(part_sum + sum(yrecv[k, c].astype(jnp.float32) for k in range(SENS - 1)))
     zc = []
     for p in range(SPLIT):
         for c in range(2):
-            zsend[p, c] = total_data[c][p * 32 : (p + 1) * 32]
+            tsum[p, c] = total_data[c][p * 32 : (p + 1) * 32]
+            zsend[p, c] = total_data[c][p * 32 : (p + 1) * 32].astype(zsend.dtype)
     for j in (2, 1, 3):
         zc.append(
             send(zsend.at[(part + SPLIT - j) % SPLIT], zrecv.at[j - 1], zs.at[j - 1], zr.at[j - 1], part_peer(SPLIT - j))
@@ -210,7 +211,7 @@
     for copy in zc:
         copy.wait()
     for c in range(2):
-        out[c] = weight * (zsend[part, c] + zrecv[0, c] + zrecv[1, c] + zrecv[2, c])
+        out[c] = weight * (tsum[part, c] + sum(zrecv[j, c].astype(jnp.float32) for j in range(SPLIT - 1)))
 
 
 def shards(probes, green_blocks, noise_table, station_class, kappa_table, coeff_index):
@@ -220,7 +221,7 @@
     vmem = pl.BlockSpec(memory_space=pltpu.VMEM)
     result = pl.pallas_call(
         functools.partial(kernel, nfreq),
-        out_shape=jax.ShapeDtypeStruct((2, 32, 128), f32),
+        out_shape=pltpu.VMEM((2, 32, 128), f32),
         in_specs=[
             vmem, vmem, vmem, pl.BlockSpec(memory_space=pltpu.SMEM), vmem,
             pl.BlockSpec(memory_space=pl.ANY),
@@ -231,10 +232,11 @@
             pltpu.VMEM((4, 4, 2, 32, 128), bf16),
             pltpu.VMEM((2, 64, 256), bf16),
             pltpu.VMEM((2, 64, 256), bf16),
-            pltpu.VMEM((3, 2, 128, 128), f32),
-            pltpu.VMEM((3, 2, 128, 128), f32),
+            pltpu.VMEM((3, 2, 128, 128), bf16),
+            pltpu.VMEM((3, 2, 128, 128), bf16),
             pltpu.VMEM((4, 2, 32, 128), f32),
-            pltpu.VMEM((3, 2, 32, 128), f32),
+            pltpu.VMEM((4, 2, 32, 128), bf16),
+            pltpu.VMEM((3, 2, 32, 128), bf16),
             dma, dma((3,)), dma((3,)), dma((3,)), dma((3,)), dma((3,)), dma((3,)),
             dma((2,)), dma((2,)), dma((3,)), dma((3,)), dma((3,)), dma((3,)),
         ],

time: 68.3 us -> 61.2 us (0.90)
  the two profiles are of different devices: /device:TPU:128 before, /device:TPU:30 now
where the time goes in v2:
time: 61.2 us; the launch traced here: 61 us
  Pallas kernels  60.3 us (99%)
  local copies, waits for them, and re-layouts  0.62 us (1%)
    pallas_call x1, Pallas kernels, shards(): pl.pallas_call(functools.partial(kernel, nfreq), out_shape=pltpu.VMEM((2,...  60.3 us

profile of v2, /device:TPU:30, one launch (start us, length us, event | category | flops | bytes accessed | tf_op | source)
XLA Modules:
  0.0 61.0 jit_solution(4003831321516693350)
XLA Ops:
  0.0 60.3 %shard_map.64 = f32[2,32,128]{2,1,0:T(8,128)S(1)} custom-call(bf16[2,32,128]{2,1,0:T(8,128)(2,1)} %bitcast.6, f32[8,64]{1,0:T(8,128)} %bitcast.8, s32[1,128]{1,0:T(1,128)} %bitcast.9, f32[16]{0:T(128)} %kappa.1, s32[32,128]{1,0:T(8,128)} %bitcast.7, bf16[2,1024,128]{2,1,0:T(8,128)(2,1)} %green.1), custom_call_target="tpu_custom_call" | custom-call | tf_op jit(solution)/shard_map/pallas_call | solution.py:222
  60.4 0.6 %copy.8 = f32[2,128,32]{1,2,0:T(8,128)} copy(f32[2,128,32]{1,2,0:T(8,128)S(1)} %bitcast.5) | data formatting | bytes 65536

commit v3 on v1

v3 whole, which is shorter than its diff:
```python
import functools

import jax
import jax.numpy as jnp
from jax import lax
from jax.experimental import pallas as pl
from jax.experimental.pallas import tpu as pltpu
from jax.sharding import PartitionSpec as P

SPLIT = 4
SENS = 4
DIP = 32
EDGE = 64
LANES = 128
MESH = pl.DeviceIdType.MESH
NT = (((1,), (1,)), ((), ()))
NEAR_FIRST = (1, 3, 2)


def kernel(
    nfreq, probes_hbm, noise_hbm, station_hbm, kappa_hbm, coeff_hbm, green, out,
    probes, noise, station, kappa, coeff, gbuf, zbuf, hsend, hrecv, ysend, yrecv, tsum, zsend, zrecv,
    in_sem, own_sem, answer, gs, gr, zys, zyr, cs, cr, hs, hr, ys, yr, zs, zr,
):
    sens = lax.axis_index("sens")
    par = lax.axis_index("par")
    part = par // nfreq
    freq = par % nfreq

    def sens_peer(k):
        return {"sens": (sens + k) % SENS, "par": par}

    def in_part(p):
        return {"sens": sens, "par": p * nfreq + freq}

    right, left = in_part((part + 1) % SPLIT), in_part((part + SPLIT - 1) % SPLIT)

    def block_of(s):
        return s + part % 2 * (SENS - 1 - 2 * s)

    def signal(sem, device):
        pl.semaphore_signal(sem, inc=1, device_id=device, device_id_type=MESH)

    def remote(src, dst, ssem, rsem, device):
        return pltpu.make_async_remote_copy(
            src_ref=src, dst_ref=dst, send_sem=ssem, recv_sem=rsem,
            device_id=device, device_id_type=MESH,
        )

    def send(*args):
        copy = remote(*args)
        copy.start()
        return copy

    barrier = pltpu.get_barrier_semaphore()
    for k in NEAR_FIRST:
        signal(barrier, sens_peer(k))

    @pl.when(part < SPLIT - 1)
    def _():
        signal(barrier, right)

    @pl.when(part == 0)
    def _():
        signal(barrier, left)

    inputs = [
        pltpu.make_async_copy(src, dst, in_sem.at[i])
        for i, (src, dst) in enumerate(
            ((noise_hbm, noise), (station_hbm, station), (probes_hbm, probes), (coeff_hbm, coeff), (kappa_hbm, kappa))
        )
    ]
    for copy in inputs:
        copy.start()
    cells = gbuf.shape[2]
    block = block_of(sens)
    own = pltpu.make_async_copy(
        green.at[:, pl.ds(pl.multiple_of(block * cells, cells), cells), :], gbuf.at[0], own_sem
    )
    own.start()
    for copy in inputs:
        copy.wait()

    lane = lax.broadcasted_iota(jnp.int32, noise.shape, 1)
    column = jnp.sum(jnp.where(lane == freq, noise[...], 0.0), axis=1, keepdims=True)
    group = lax.broadcasted_iota(jnp.int32, (noise.shape[0], station.shape[1]), 0)
    variance = jnp.sum(jnp.where(group == station[...], column, 0.0), axis=0, keepdims=True)
    weight = 1.0 / jnp.sqrt(variance)
    for c in range(2):
        zbuf[part, 0, c] = (weight * probes[c].astype(jnp.float32)).astype(jnp.bfloat16)

    pl.semaphore_wait(barrier, SENS - 1 + (part + 3) // 4 + part // 3)

    @pl.when(part > 0)
    def _():
        signal(answer.at[0], left)

    @pl.when(part == SPLIT - 1)
    def _():
        signal(answer.at[1], right)

    zy = {
        k: send(zbuf.at[part, 0], zbuf.at[part, k], zys.at[k - 1], zyr.at[k - 1], sens_peer(k))
        for k in NEAR_FIRST
    }
    g = {}
    spans = ((0, EDGE), (cells - EDGE, EDGE), (EDGE, cells - 2 * EDGE))
    for which in ((0, 1), (2,)):
        for k in NEAR_FIRST:
            theirs = block_of((sens + k) % SENS) * cells
            for e in which:
                first, count = spans[e]
                rows = pl.ds(pl.multiple_of(theirs + first, EDGE), count)
                g[k, e] = send(
                    green.at[:, rows, :], gbuf.at[k, :, pl.ds(first, count), :],
                    gs.at[k - 1, e], gr.at[k - 1, e], sens_peer(k),
                )

    place = part * SENS + block
    total = SPLIT * SENS
    rows_all = coeff.shape[0]

    def inverse(row, keep):
        index = coeff[pl.ds((row + rows_all) % rows_all, 1), :]
        value = jnp.zeros(index.shape, jnp.float32)
        for n in range(kappa.shape[0]):
            value = jnp.where(index == n, kappa[n], value)
        value = jnp.where(keep, 1.0 / (4.0 + value), 0.0)
        return jnp.broadcast_to(value, (LANES, LANES)).T

    before = inverse(2 * place - 1, place > 0)
    after = inverse(2 * place + 2, place < total - 1)
    inv = jnp.concatenate(
        [before[EDGE:], inverse(2 * place, True), inverse(2 * place + 1, True), after[:EDGE]], axis=0
    ).reshape(12, DIP, LANES)

    @pl.when(place == 0)
    def _():
        for h in range(2):
            hrecv[h, 0] = jnp.zeros(hrecv.shape[2:], hrecv.dtype)

    @pl.when(place == total - 1)
    def _():
        for h in range(2):
            hrecv[h, 1] = jnp.zeros(hrecv.shape[2:], hrecv.dtype)

    def probe_copy(way, c, k):
        spot = zbuf.at[c, k]
        return remote(spot, spot, cs.at[way, c, k], cr.at[c, k], (right, left)[way])

    order = (0, *NEAR_FIRST)

    def pass_on(way, c):
        for k in order:
            probe_copy(way, c, k).start()

    def arrived(c):
        for k in order:
            probe_copy(0, c, k).wait_recv()

    def relay(way, c):
        for k in order:
            probe_copy(0, c, k).wait_recv()
            probe_copy(way, c, k).start()

    def pass_own(ways, c):
        for k in order:
            if k > 0:
                zy[k].wait_recv()
            for way in ways:
                probe_copy(way, c, k).start()

    @pl.when(part == 0)
    def _():
        pl.semaphore_wait(answer.at[0], 1)
        pass_own((0,), 0)
        arrived(1)
        pl.semaphore_wait(answer.at[1], 1)
        pass_on(1, 0)
        pass_on(1, 1)

    @pl.when(part == 1)
    def _():
        pass_own((1,), 1)
        arrived(0)
        pl.semaphore_wait(answer.at[0], 1)
        pass_on(0, 1)
        pass_on(0, 0)

    @pl.when(part == 2)
    def _():
        pass_own((1,), 2)
        pl.semaphore_wait(answer.at[0], 1)
        pass_on(0, 2)
        arrived(1)
        arrived(0)

    @pl.when(part == 3)
    def _():
        pass_own((0, 1), 3)
        arrived(0)
        arrived(1)

    def probe_rows(h, k):
        z_re = zbuf[2 * h : 2 * h + 2, k, 0].reshape(EDGE, LANES)
        z_im = zbuf[2 * h : 2 * h + 2, k, 1].reshape(EDGE, LANES)
        return jnp.concatenate(
            [jnp.concatenate([z_re, z_im], axis=1), jnp.concatenate([z_im, -z_re], axis=1)], axis=0
        )

    def source(h, spans_of):
        result = 0.0
        for k in order:
            a = jnp.concatenate(
                [
                    jnp.concatenate([gbuf[k, c, pl.ds(first, count), :] for c in range(2)], axis=1)
                    for first, count in spans_of
                ],
                axis=0,
            )
            result += lax.dot_general(a, probe_rows(h, k), NT, preferred_element_type=jnp.float32)
        return result

    def device_of(b):
        p = b // SENS
        r = b % SENS
        return {"sens": r + p % 2 * (SENS - 1 - 2 * r), "par": p * nfreq + freq}

    def rim(h, side):
        other = device_of((place + (total - 1, 1)[side]) % total)
        return remote(hsend.at[h, side], hrecv.at[h, 1 - side], hs.at[h, side], hr.at[h, 1 - side], other)

    def edges(h):
        src = source(h, spans[:2])
        hsend[h, 0] = src[:EDGE].astype(jnp.bfloat16)
        hsend[h, 1] = src[EDGE:].astype(jnp.bfloat16)

        @pl.when(place > 0)
        def _():
            rim(h, 0).start()

        @pl.when(place < total - 1)
        def _():
            rim(h, 1).start()

        return src

    own.wait()
    for k in NEAR_FIRST:
        for e in (0, 1):
            g[k, e].wait_recv()
    edge = [edges(0)]

    @pl.when(part == 0)
    def _():
        relay(0, 3)
        arrived(2)

    @pl.when(part == 1)
    def _():
        relay(1, 2)
        arrived(3)

    @pl.when(part == 2)
    def _():
        arrived(3)

    @pl.when(part == 3)
    def _():
        arrived(2)

    edge.append(edges(1))
    for k in NEAR_FIRST:
        g[k, 2].wait_recv()
    middle = [source(h, spans[2:]) for h in range(2)]

    def dips(u):
        zero = jnp.zeros((u.shape[0], 1, u.shape[2]), u.dtype)
        return jnp.concatenate([u[:, 1:], zero], axis=1) + jnp.concatenate([zero, u[:, :-1]], axis=1)

    def sum_copy(c, k):
        return remote(
            ysend.at[k - 1, c], yrecv.at[k - 1, c], ys.at[c, k - 1], yr.at[c, k - 1], sens_peer(SENS - k)
        )

    for h in range(2):
        @pl.when(place > 0)
        def _():
            remote(hsend.at[h, 1], hrecv.at[h, 0], hs.at[h, 1], hr.at[h, 0], left).wait_recv()

        @pl.when(place < total - 1)
        def _():
            remote(hsend.at[h, 0], hrecv.at[h, 1], hs.at[h, 0], hr.at[h, 1], left).wait_recv()

        full = jnp.concatenate(
            [
                hrecv[h, 0].astype(jnp.float32), edge[h][:EDGE], middle[h], edge[h][EDGE:],
                hrecv[h, 1].astype(jnp.float32),
            ],
            axis=0,
        ).reshape(12, DIP, LANES)
        u1 = full * inv
        u2 = (full[1:11] + u1[:10] + u1[2:] + dips(u1[1:11])) * inv[1:11]
        slip = (full[2:10] + u2[:8] + u2[2:] + dips(u2[1:9])) * inv[2:10]
        slip_t = slip.reshape(cells, LANES).astype(jnp.bfloat16).T

        for k in (*NEAR_FIRST, 0):
            b = jnp.concatenate([gbuf[k, 0], gbuf[k, 1]], axis=1)
            both = jnp.dot(slip_t, b, preferred_element_type=jnp.float32)
            re = both[:EDGE, :LANES] - both[EDGE:, LANES:]
            im = both[EDGE:, :LANES] + both[:EDGE, LANES:]
            for c, value in ((0, re), (1, im)):
                for i in range(2):
                    piece = value[i * 32 : (i + 1) * 32]
                    if k == 0:
                        tsum[2 * h + i, c] = piece
                    else:
                        ysend[k - 1, 2 * h + i, c] = piece.astype(ysend.dtype)
        for i in range(2):
            for k in NEAR_FIRST:
                sum_copy(2 * h + i, k).start()

    def sens_sum(p, c):
        return tsum[p, c] + sum(yrecv[k, p, c].astype(jnp.float32) for k in range(SENS - 1))

    def share(c):
        slot = (part - c + SPLIT) % SPLIT - 1
        return remote(zsend.at[c], zrecv.at[slot], zs.at[c], zr.at[slot], in_part(c))

    for p in range(SPLIT):
        for k in NEAR_FIRST:
            sum_copy(p, k).wait_recv()

        @pl.when(part != p)
        def _():
            for c in range(2):
                zsend[p, c] = sens_sum(p, c).astype(zsend.dtype)
            share(p).start()

    mine = [sens_sum(part, c) for c in range(2)]
    for j in range(SPLIT - 1):
        remote(zsend.at[0], zrecv.at[j], zs.at[0], zr.at[j], left).wait_recv()
    for c in range(2):
        out[c] = weight * (mine[c] + sum(zrecv[j, c].astype(jnp.float32) for j in range(SPLIT - 1)))

    for copy in [*zy.values(), *g.values()]:
        copy.wait_send()

    def gone(way, c):
        for k in order:
            probe_copy(way, c, k).wait_send()

    for p, sent in enumerate((((0, 0), (1, 0), (1, 1), (0, 3)), ((1, 1), (0, 1), (0, 0), (1, 2)), ((1, 2), (0, 2)), ((0, 3), (1, 3)))):

        @pl.when(part == p)
        def _():
            for way, c in sent:
                gone(way, c)

    for h in range(2):

        @pl.when(place > 0)
        def _():
            rim(h, 0).wait_send()

        @pl.when(place < total - 1)
        def _():
            rim(h, 1).wait_send()

    for p in range(SPLIT):
        for k in NEAR_FIRST:
            sum_copy(p, k).wait_send()

        @pl.when(part != p)
        def _():
            share(p).wait_send()


def shards(probes, green_blocks, noise_table, station_class, kappa_table, coeff_index):
    nfreq = noise_table.shape[0]
    bf16, f32, i32 = jnp.bfloat16, jnp.float32, jnp.int32
    dma = pltpu.SemaphoreType.DMA
    coeff = coeff_index.reshape(-1, LANES)
    hbm = pl.BlockSpec(memory_space=pl.ANY)
    result = pl.pallas_call(
        functools.partial(kernel, nfreq),
        out_shape=pltpu.VMEM((2, 32, LANES), f32),
        in_specs=[hbm] * 6,
        out_specs=pl.BlockSpec(memory_space=pltpu.VMEM),
        scratch_shapes=[
            pltpu.VMEM((2, 32, LANES), bf16),
            pltpu.VMEM(noise_table.shape[::-1], f32),
            pltpu.VMEM((1, LANES), i32),
            pltpu.SMEM(kappa_table.shape, f32),
            pltpu.VMEM(coeff.shape, i32),
            pltpu.VMEM((4, 2, 256, LANES), bf16),
            pltpu.VMEM((4, 4, 2, 32, LANES), bf16),
            pltpu.VMEM((2, 2, EDGE, LANES), bf16),
            pltpu.VMEM((2, 2, EDGE, LANES), bf16),
            pltpu.VMEM((3, 4, 2, 32, LANES), bf16),
            pltpu.VMEM((3, 4, 2, 32, LANES), bf16),
            pltpu.VMEM((4, 2, 32, LANES), f32),
            pltpu.VMEM((4, 2, 32, LANES), bf16),
            pltpu.VMEM((3, 2, 32, LANES), bf16),
            dma((5,)), dma, pltpu.SemaphoreType.REGULAR((2,)),
            dma((3, 3)), dma((3, 3)), dma((3,)), dma((3,)), dma((2, 4, 4)), dma((4, 4)),
            dma((2, 2)), dma((2, 2)), dma((4, 3)), dma((4, 3)), dma((4,)), dma((3,)),
        ],
        compiler_params=pltpu.CompilerParams(collective_id=0, has_side_effects=True),
    )(
        probes.transpose(0, 2, 1), noise_table.T, station_class.reshape(1, -1), kappa_table,
        coeff, green_blocks,
    )
    return result.transpose(0, 2, 1)


def solution(mesh):
    in_specs = (P(None, "sens", "par"), P(None, "par", "sens"), P(), P("sens"), P(), P())
    out_specs = P(None, "sens", "par")
    return jax.shard_map(shards, mesh=mesh, in_specs=in_specs, out_specs=out_specs, check_vma=False)
```

time: 68.3 us -> 56.1 us (0.82)
  the two profiles are of different devices: /device:TPU:128 before, /device:TPU:134 now
where the time goes in v3:
time: 56.1 us; the launch traced here: 55.9 us
  Pallas kernels  55.3 us (99%)
  local copies, waits for them, and re-layouts  0.62 us (1%)
    pallas_call x1, Pallas kernels, shards(): pl.pallas_call(functools.partial(kernel, nfreq), out_shape=pltpu.VMEM((2,...  55.3 us

profile of v3, /device:TPU:134, one launch (start us, length us, event | category | flops | bytes accessed | tf_op | source)
XLA Modules:
  0.0 55.9 jit_solution(17507843669073268137)
XLA Ops:
  0.0 55.3 %shard_map.64 = f32[2,32,128]{2,1,0:T(8,128)S(1)} custom-call(bf16[2,32,128]{2,1,0:T(8,128)(2,1)} %bitcast.6, f32[8,64]{1,0:T(8,128)} %bitcast.8, s32[1,128]{1,0:T(1,128)} %bitcast.9, f32[16]{0:T(128)} %kappa_hbm.1, s32[32,128]{1,0:T(8,128)} %bitcast.7, bf16[2,1024,128]{2,1,0:T(8,128)(2,1)} %green.1), custom_call_target="tpu_custom_call" | custom-call | tf_op jit(solution)/shard_map/pallas_call | solution.py:385
  55.3 0.6 %copy.8 = f32[2,128,32]{1,2,0:T(8,128)} copy(f32[2,128,32]{1,2,0:T(8,128)S(1)} %bitcast.5) | data formatting | bytes 65536

commit v4 on v2

--- a/solution.py
+++ b/solution.py
@@ -15,9 +15,9 @@
 
 
 def kernel(
-    nfreq, probes, noise, station, kappa, coeff, green, out,
-    gbuf, zbuf, hsend, hrecv, ysend, yrecv, tsum, zsend, zrecv,
-    own_sem, gs, gr, zys, zyr, zzs, zzr, hs, hr, ys, yr, zs, zr,
+    nfreq, probes_hbm, noise_hbm, station_hbm, kappa_hbm, coeff_hbm, green, out,
+    probes, noise, station, kappa, coeff, in_sem, gbuf, zbuf, hsend, hrecv, ysend, yrecv, tsum, zsend, zrecv,
+    own_sem, gs, gr, zys, zyr, rs, rr, ls, lr, fs, fr, hs, hr, ys, yr, zs, zr,
 ):
     sens = lax.axis_index("sens")
     par = lax.axis_index("par")
@@ -44,15 +44,26 @@
     barrier = pltpu.get_barrier_semaphore()
     for k in range(1, SENS):
         pl.semaphore_signal(barrier, inc=1, device_id=sens_peer(k), device_id_type=MESH)
-    for j in range(1, SPLIT):
+    for j in (1, SPLIT - 1):
         pl.semaphore_signal(barrier, inc=1, device_id=part_peer(j), device_id_type=MESH)
 
+    inputs = [
+        pltpu.make_async_copy(src, dst, in_sem.at[i])
+        for i, (src, dst) in enumerate(
+            ((noise_hbm, noise), (station_hbm, station), (probes_hbm, probes), (coeff_hbm, coeff), (kappa_hbm, kappa))
+        )
+    ]
+    for copy in inputs:
+        copy.start()
     cells = gbuf.shape[2]
     block = block_of(sens)
     own = pltpu.make_async_copy(
         green.at[:, pl.ds(pl.multiple_of(block * cells, cells), cells), :], gbuf.at[0], own_sem
     )
     own.start()
+
+    for copy in inputs:
+        copy.wait()
 
     lane = lax.broadcasted_iota(jnp.int32, noise.shape, 1)
     column = jnp.sum(jnp.where(lane == freq, noise[...], 0.0), axis=1, keepdims=True)
@@ -62,17 +73,43 @@
     for c in range(2):
         zbuf[part, 0, c] = (weight * probes[c].astype(jnp.float32)).astype(jnp.bfloat16)
 
-    pl.semaphore_wait(barrier, SENS - 1 + SPLIT - 1)
-
-    zy = [
-        send(zbuf.at[part, 0], zbuf.at[part, k], zys.at[k - 1], zyr.at[k - 1], sens_peer(k))
-        for k in range(1, SENS)
-    ]
-    g = []
-    for k in (1, 3, 2):
+    pl.semaphore_wait(barrier, SENS - 1 + 2)
+
+    right, left = (part + 1) % SPLIT, (part + 3) % SPLIT
+    zy = {
+        k: send(zbuf.at[part, 0], zbuf.at[part, k], zys.at[k - 1], zyr.at[k - 1], sens_peer(k))
+        for k in (1, 3, 2)
+    }
+
+    def both_ways(k):
+        block = zbuf.at[part, k]
+        return (
+            send(block, block, rs.at[k], rr.at[k], part_peer(1)),
+            send(block, block, ls.at[k], lr.at[k], part_peer(3)),
+        )
+
+    ways = {0: both_ways(0)}
+    core = par % 2
+
+    def green_copy(k):
         theirs = block_of((sens + k) % SENS)
         rows = pl.ds(pl.multiple_of(theirs * cells, cells), cells)
-        g.append(send(green.at[:, rows, :], gbuf.at[k], gs.at[k - 1], gr.at[k - 1], sens_peer(k)))
+        return pltpu.make_async_remote_copy(
+            src_ref=green.at[:, rows, :], dst_ref=gbuf.at[k], send_sem=gs.at[k - 1], recv_sem=gr.at[k - 1],
+            device_id=sens_peer(k), device_id_type=MESH,
+        )
+
+    g = {k: green_copy(k) for k in (1, 3, 2)}
+
+    @pl.when(core == 0)
+    def _():
+        for k in (1, 3, 2):
+            g[k].start()
+
+    @pl.when(core == 1)
+    def _():
+        for k in ():
+            g[k].start()
 
     place = part * SENS + block
     rows_all = coeff.shape[0]
@@ -95,30 +132,55 @@
     inv = inv.reshape(12, DIP, 128)
     inv = jnp.concatenate([inv, inv], axis=2)
 
-    for copy in zy:
-        copy.wait()
-    zz = [
-        send(zbuf.at[part], zbuf.at[part], zzs.at[j - 1], zzr.at[j - 1], part_peer(j))
-        for j in range(1, SPLIT)
-    ]
-    own.wait()
-    for copy in zz:
-        copy.wait()
-    for copy in g:
-        copy.wait()
-
-    src = jnp.zeros((cells, 256), jnp.float32)
-    for k in range(SENS):
-        a = jnp.concatenate([gbuf[k, 0], gbuf[k, 1]], axis=1)
+    for k in (1, 3, 2):
+        zy[k].wait_recv()
+        ways[k] = both_ways(k)
+    @pl.when(core == 1)
+    def _():
+        for k in (1, 3, 2):
+            g[k].start()
+
+    passed = {}
+    for k in (0, 1, 3, 2):
+        to_right, to_left = ways[k]
+        if k in (0, 3):
+            to_right.wait_recv()
+            block = zbuf.at[left, k]
+            passed[k] = send(block, block, fs.at[k], fr.at[k], part_peer(1))
+        else:
+            to_left.wait_recv()
+            block = zbuf.at[right, k]
+            passed[k] = send(block, block, fs.at[k], fr.at[k], part_peer(3))
+
+    def probe_rows(k):
         z_re = zbuf[:, k, 0].reshape(128, 128)
         z_im = zbuf[:, k, 1].reshape(128, 128)
-        b = jnp.concatenate(
+        return jnp.concatenate(
             [jnp.concatenate([z_re, z_im], axis=1), jnp.concatenate([z_im, -z_re], axis=1)], axis=0
         )
-        src += lax.dot_general(a, b, NT, preferred_element_type=jnp.float32)
-
-    hsend[0] = src[:64].astype(jnp.bfloat16)
-    hsend[1] = src[cells - 64 :].astype(jnp.bfloat16)
+
+    def source(k, *spans):
+        a = jnp.concatenate(
+            [
+                jnp.concatenate([gbuf[k, c, pl.ds(first, count), :] for c in range(2)], axis=1)
+                for first, count in spans
+            ],
+            axis=0,
+        )
+        return lax.dot_general(a, probe_rows(k), NT, preferred_element_type=jnp.float32)
+
+    edge = 0.0
+    for k in (0, 1, 3, 2):
+        if k == 0:
+            own.wait()
+        else:
+            g[k].wait_recv()
+        ways[k][1 if k in (0, 3) else 0].wait_recv()
+        passed[k].wait_recv()
+        edge += source(k, (0, 64), (cells - 64, 64))
+
+    hsend[0] = edge[:64].astype(jnp.bfloat16)
+    hsend[1] = edge[64:].astype(jnp.bfloat16)
 
     def device_of(b):
         p = b // SENS
@@ -140,6 +202,8 @@
     @pl.when(place < total - 1)
     def _():
         rim(1, (place + 1) % total).start()
+
+    middle = sum(source(k, (64, cells - 128)) for k in range(SENS))
 
     @pl.when(place == 0)
     def _():
@@ -168,7 +232,11 @@
         ).wait_recv()
 
     full = jnp.concatenate(
-        [hrecv[0].astype(jnp.float32), src, hrecv[1].astype(jnp.float32)], axis=0
+        [
+            hrecv[0].astype(jnp.float32), edge[:64], middle, edge[64:],
+            hrecv[1].astype(jnp.float32),
+        ],
+        axis=0,
     ).reshape(12, DIP, 256)
 
     def dips(u):
@@ -185,33 +253,46 @@
         both = jnp.dot(slip_t, b, preferred_element_type=jnp.float32)
         return both[:128, :128] - both[128:, 128:], both[128:, :128] + both[:128, 128:]
 
-    y = []
-    for k in (2, 1, 3):
-        re, im = data_of(k)
-        ysend[k - 1, 0] = re.astype(ysend.dtype)
-        ysend[k - 1, 1] = im.astype(ysend.dtype)
-        y.append(
-            send(ysend.at[k - 1], yrecv.at[k - 1], ys.at[k - 1], yr.at[k - 1], sens_peer(SENS - k))
-        )
-    re, im = data_of(0)
-    for copy in y:
-        copy.wait()
-    total_data = []
-    for c, part_sum in ((0, re), (1, im)):
-        total_data.append(part_sum + sum(yrecv[k, c].astype(jnp.float32) for k in range(SENS - 1)))
-    zc = []
-    for p in range(SPLIT):
+    for k in range(SENS):
+        for c, value in enumerate(data_of(k)):
+            for p in range(SPLIT):
+                piece = value[p * 32 : (p + 1) * 32]
+                if k == 0:
+                    tsum[p, c] = piece
+                else:
+                    ysend[k - 1, p, c] = piece.astype(ysend.dtype)
+
+    y = {}
+    for j in (2, 1, 3, 0):
+        p = (part + j) % SPLIT
+        for k in (2, 1, 3):
+            y[j, k] = send(
+                ysend.at[k - 1, p], yrecv.at[k - 1, p], ys.at[k - 1, j], yr.at[k - 1, j], sens_peer(SENS - k)
+            )
+
+    def sens_sum(j, c):
+        p = (part + j) % SPLIT
+        return tsum[p, c] + sum(yrecv[k, p, c].astype(jnp.float32) for k in range(SENS - 1))
+
+    z = []
+    for j in (2, 1, 3):
+        for k in (1, 3, 2):
+            y[j, k].wait_recv()
         for c in range(2):
-            tsum[p, c] = total_data[c][p * 32 : (p + 1) * 32]
-            zsend[p, c] = total_data[c][p * 32 : (p + 1) * 32].astype(zsend.dtype)
-    for j in (2, 1, 3):
-        zc.append(
-            send(zsend.at[(part + SPLIT - j) % SPLIT], zrecv.at[j - 1], zs.at[j - 1], zr.at[j - 1], part_peer(SPLIT - j))
-        )
-    for copy in zc:
-        copy.wait()
+            zsend[j - 1, c] = sens_sum(j, c).astype(zsend.dtype)
+        z.append(send(zsend.at[j - 1], zrecv.at[j - 1], zs.at[j - 1], zr.at[j - 1], part_peer(j)))
+    for k in (1, 3, 2):
+        y[0, k].wait_recv()
+    mine = [sens_sum(0, c) for c in range(2)]
+    for copy in z:
+        copy.wait_recv()
     for c in range(2):
-        out[c] = weight * (tsum[part, c] + sum(zrecv[j, c].astype(jnp.float32) for j in range(SPLIT - 1)))
+        out[c] = weight * (mine[c] + sum(zrecv[j, c].astype(jnp.float32) for j in range(SPLIT - 1)))
+    for copy in [*zy.values(), *g.values(), *passed.values(), *y.values(), *z]:
+        copy.wait_send()
+    for pair in ways.values():
+        for copy in pair:
+            copy.wait_send()
 
 
 def shards(probes, green_blocks, noise_table, station_class, kappa_table, coeff_index):
@@ -222,23 +303,27 @@
     result = pl.pallas_call(
         functools.partial(kernel, nfreq),
         out_shape=pltpu.VMEM((2, 32, 128), f32),
-        in_specs=[
-            vmem, vmem, vmem, pl.BlockSpec(memory_space=pltpu.SMEM), vmem,
-            pl.BlockSpec(memory_space=pl.ANY),
-        ],
+        in_specs=[pl.BlockSpec(memory_space=pl.ANY)] * 6,
         out_specs=vmem,
         scratch_shapes=[
+            pltpu.VMEM((2, 32, 128), bf16),
+            pltpu.VMEM(noise_table.shape[::-1], f32),
+            pltpu.VMEM((1, 128), jnp.int32),
+            pltpu.SMEM(kappa_table.shape, f32),
+            pltpu.VMEM((32, 128), jnp.int32),
+            dma((5,)),
             pltpu.VMEM((4, 2, 256, 128), bf16),
             pltpu.VMEM((4, 4, 2, 32, 128), bf16),
             pltpu.VMEM((2, 64, 256), bf16),
             pltpu.VMEM((2, 64, 256), bf16),
-            pltpu.VMEM((3, 2, 128, 128), bf16),
-            pltpu.VMEM((3, 2, 128, 128), bf16),
+            pltpu.VMEM((3, 4, 2, 32, 128), bf16),
+            pltpu.VMEM((3, 4, 2, 32, 128), bf16),
             pltpu.VMEM((4, 2, 32, 128), f32),
-            pltpu.VMEM((4, 2, 32, 128), bf16),
             pltpu.VMEM((3, 2, 32, 128), bf16),
-            dma, dma((3,)), dma((3,)), dma((3,)), dma((3,)), dma((3,)), dma((3,)),
-            dma((2,)), dma((2,)), dma((3,)), dma((3,)), dma((3,)), dma((3,)),
+            pltpu.VMEM((3, 2, 32, 128), bf16),
+            dma, dma((3,)), dma((3,)), dma((3,)), dma((3,)),
+            dma((4,)), dma((4,)), dma((4,)), dma((4,)), dma((4,)), dma((4,)),
+            dma((2,)), dma((2,)), dma((3, 4)), dma((3, 4)), dma((3,)), dma((3,)),
         ],
         compiler_params=pltpu.CompilerParams(collective_id=0, has_side_effects=True),
     )(

time: 61.2 us -> 54.4 us (0.89)
  the two profiles are of different devices: /device:TPU:30 before, /device:TPU:68 now
where the time goes in v4:
time: 54.4 us; the launch traced here: 54.3 us
  Pallas kernels  53.6 us (99%)
  local copies, waits for them, and re-layouts  0.62 us (1%)
    pallas_call x1, Pallas kernels, shards(): pl.pallas_call(functools.partial(kernel, nfreq), out_shape=pltpu.VMEM((2,...  53.6 us

profile of v4, /device:TPU:68, one launch (start us, length us, event | category | flops | bytes accessed | tf_op | source)
XLA Modules:
  0.0 54.3 jit_solution(17276709189022392387)
XLA Ops:
  0.0 53.6 %shard_map.64 = f32[2,32,128]{2,1,0:T(8,128)S(1)} custom-call(bf16[2,32,128]{2,1,0:T(8,128)(2,1)} %bitcast.6, f32[8,64]{1,0:T(8,128)} %bitcast.8, s32[1,128]{1,0:T(1,128)} %bitcast.9, f32[16]{0:T(128)} %kappa_hbm.1, s32[32,128]{1,0:T(8,128)} %bitcast.7, bf16[2,1024,128]{2,1,0:T(8,128)(2,1)} %green.1), custom_call_target="tpu_custom_call" | custom-call | tf_op jit(solution)/shard_map/pallas_call | solution.py:303
  53.6 0.6 %copy.8 = f32[2,128,32]{1,2,0:T(8,128)} copy(f32[2,128,32]{1,2,0:T(8,128)S(1)} %bitcast.5) | data formatting | bytes 65536

commit v5 on v4

--- a/solution.py
+++ b/solution.py
@@ -205,6 +205,22 @@
 
     middle = sum(source(k, (64, cells - 128)) for k in range(SENS))
 
+    def dips(u):
+        zero = jnp.zeros((u.shape[0], 1, u.shape[2]), u.dtype)
+        return jnp.concatenate([u[:, 1:], zero], axis=1) + jnp.concatenate([zero, u[:, :-1]], axis=1)
+
+    own_src = jnp.concatenate([edge[:64], middle, edge[64:]], axis=0).reshape(8, DIP, 256)
+    inv_o = inv[2:10]
+    u1 = own_src * inv_o
+    none = jnp.zeros((1, DIP, 256), jnp.float32)
+    base2 = (
+        own_src + jnp.concatenate([none, u1[:-1]], axis=0) + jnp.concatenate([u1[1:], none], axis=0) + dips(u1)
+    )
+    u2 = base2[1:7] * inv_o[1:7]
+    slip = (own_src[2:6] + u2[:4] + u2[2:] + dips(u2[1:5])) * inv_o[2:6]
+    inner_t = slip.reshape(128, 256).astype(jnp.bfloat16).T
+
+
     @pl.when(place == 0)
     def _():
         hrecv[0] = jnp.zeros(hrecv.shape[1:], hrecv.dtype)
@@ -231,25 +247,31 @@
             recv_sem=hr.at[1], device_id=device_of((place + 1) % total), device_id_type=MESH,
         ).wait_recv()
 
-    full = jnp.concatenate(
+    rim_l, rim_r = (hrecv[side].astype(jnp.float32).reshape(2, DIP, 256) for side in range(2))
+    u1_l, u1_r = rim_l * inv[:2], rim_r * inv[10:]
+    u2_0 = (base2[:1] + u1_l[1:]) * inv_o[:1]
+    u2_7 = (base2[7:] + u1_r[:1]) * inv_o[7:]
+    u2_l = (rim_l[1:] + u1_l[:1] + u1[:1] + dips(u1_l[1:])) * inv[1:2]
+    u2_r = (rim_r[:1] + u1_r[1:] + u1[7:] + dips(u1_r[:1])) * inv[10:11]
+    outer = jnp.concatenate(
         [
-            hrecv[0].astype(jnp.float32), edge[:64], middle, edge[64:],
-            hrecv[1].astype(jnp.float32),
+            (own_src[:1] + u2_l + u2[:1] + dips(u2_0)) * inv_o[:1],
+            (own_src[1:2] + u2_0 + u2[1:2] + dips(u2[:1])) * inv_o[1:2],
+            (own_src[6:7] + u2[4:5] + u2_7 + dips(u2[5:])) * inv_o[6:7],
+            (own_src[7:] + u2[5:] + u2_r + dips(u2_7)) * inv_o[7:],
         ],
         axis=0,
-    ).reshape(12, DIP, 256)
-
-    def dips(u):
-        zero = jnp.zeros((u.shape[0], 1, u.shape[2]), u.dtype)
-        return jnp.concatenate([u[:, 1:], zero], axis=1) + jnp.concatenate([zero, u[:, :-1]], axis=1)
-
-    u1 = full * inv
-    u2 = (full[1:11] + u1[:10] + u1[2:] + dips(u1[1:11])) * inv[1:11]
-    slip = (full[2:10] + u2[:8] + u2[2:] + dips(u2[1:9])) * inv[2:10]
-    slip_t = slip.reshape(cells, 256).astype(jnp.bfloat16).T
+    )
+    slip_t = jnp.concatenate([inner_t, outer.reshape(128, 256).astype(jnp.bfloat16).T], axis=1)
 
     def data_of(k):
-        b = jnp.concatenate([gbuf[k, 0], gbuf[k, 1]], axis=1)
+        b = jnp.concatenate(
+            [
+                jnp.concatenate([gbuf[k, c, pl.ds(first, count), :] for c in range(2)], axis=1)
+                for first, count in ((64, cells - 128), (0, 64), (cells - 64, 64))
+            ],
+            axis=0,
+        )
         both = jnp.dot(slip_t, b, preferred_element_type=jnp.float32)
         return both[:128, :128] - both[128:, 128:], both[128:, :128] + both[:128, 128:]
 

time: 54.4 us -> 54.2 us (level)
  the two profiles are of different devices: /device:TPU:68 before, /device:TPU:70 now
where the time goes in v5:
time: 54.2 us; the launch traced here: 54.1 us
  Pallas kernels  53.4 us (99%)
  local copies, waits for them, and re-layouts  0.62 us (1%)
    pallas_call x1, Pallas kernels, shards(): pl.pallas_call(functools.partial(kernel, nfreq), out_shape=pltpu.VMEM((2,...  53.4 us

profile of v5, /device:TPU:70, one launch (start us, length us, event | category | flops | bytes accessed | tf_op | source)
XLA Modules:
  0.0 54.1 jit_solution(14836124982413597860)
XLA Ops:
  0.0 53.4 %shard_map.64 = f32[2,32,128]{2,1,0:T(8,128)S(1)} custom-call(bf16[2,32,128]{2,1,0:T(8,128)(2,1)} %bitcast.6, f32[8,64]{1,0:T(8,128)} %bitcast.8, s32[1,128]{1,0:T(1,128)} %bitcast.9, f32[16]{0:T(128)} %kappa_hbm.1, s32[32,128]{1,0:T(8,128)} %bitcast.7, bf16[2,1024,128]{2,1,0:T(8,128)(2,1)} %green.1), custom_call_target="tpu_custom_call" | custom-call | tf_op jit(solution)/shard_map/pallas_call | solution.py:325
  53.4 0.6 %copy.8 = f32[2,128,32]{1,2,0:T(8,128)} copy(f32[2,128,32]{1,2,0:T(8,128)S(1)} %bitcast.5) | data formatting | bytes 65536

commit v6 on v5

--- a/solution.py
+++ b/solution.py
@@ -137,7 +137,7 @@
         ways[k] = both_ways(k)
     @pl.when(core == 1)
     def _():
-        for k in (1, 3, 2):
+        for k in (2, 1, 3):
             g[k].start()
 
     passed = {}

time: 54.2 us -> 53.6 us (0.989)
  the two profiles are of different devices: /device:TPU:70 before, /device:TPU:4 now
where the time goes in v6:
time: 53.6 us; the launch traced here: 53.4 us
  Pallas kernels  52.8 us (99%)
  local copies, waits for them, and re-layouts  0.62 us (1%)
    pallas_call x1, Pallas kernels, shards(): pl.pallas_call(functools.partial(kernel, nfreq), out_shape=pltpu.VMEM((2,...  52.8 us

profile of v6, /device:TPU:4, one launch (start us, length us, event | category | flops | bytes accessed | tf_op | source)
XLA Modules:
  0.0 53.4 jit_solution(8691551184307629354)
XLA Ops:
  0.0 52.8 %shard_map.64 = f32[2,32,128]{2,1,0:T(8,128)S(1)} custom-call(bf16[2,32,128]{2,1,0:T(8,128)(2,1)} %bitcast.6, f32[8,64]{1,0:T(8,128)} %bitcast.8, s32[1,128]{1,0:T(1,128)} %bitcast.9, f32[16]{0:T(128)} %kappa_hbm.1, s32[32,128]{1,0:T(8,128)} %bitcast.7, bf16[2,1024,128]{2,1,0:T(8,128)(2,1)} %green.1), custom_call_target="tpu_custom_call" | custom-call | tf_op jit(solution)/shard_map/pallas_call | solution.py:325
  52.8 0.6 %copy.8 = f32[2,128,32]{1,2,0:T(8,128)} copy(f32[2,128,32]{1,2,0:T(8,128)S(1)} %bitcast.5) | data formatting | bytes 65536

commit v7 on v6

--- a/solution.py
+++ b/solution.py
@@ -78,7 +78,7 @@
     right, left = (part + 1) % SPLIT, (part + 3) % SPLIT
     zy = {
         k: send(zbuf.at[part, 0], zbuf.at[part, k], zys.at[k - 1], zyr.at[k - 1], sens_peer(k))
-        for k in (1, 3, 2)
+        for k in (2, 1, 3)
     }
 
     def both_ways(k):

time: 53.6 us -> 56.3 us (1.050)
  the two profiles are of different devices: /device:TPU:4 before, /device:TPU:14 now
where the time goes in v7:
time: 56.3 us; the launch traced here: 56.2 us
  Pallas kernels  55.6 us (99%)
  local copies, waits for them, and re-layouts  0.62 us (1%)
    pallas_call x1, Pallas kernels, shards(): pl.pallas_call(functools.partial(kernel, nfreq), out_shape=pltpu.VMEM((2,...  55.6 us

profile of v7, /device:TPU:14, one launch (start us, length us, event | category | flops | bytes accessed | tf_op | source)
XLA Modules:
  0.0 56.2 jit_solution(9772365266493117460)
XLA Ops:
  0.0 55.6 %shard_map.64 = f32[2,32,128]{2,1,0:T(8,128)S(1)} custom-call(bf16[2,32,128]{2,1,0:T(8,128)(2,1)} %bitcast.6, f32[8,64]{1,0:T(8,128)} %bitcast.8, s32[1,128]{1,0:T(1,128)} %bitcast.9, f32[16]{0:T(128)} %kappa_hbm.1, s32[32,128]{1,0:T(8,128)} %bitcast.7, bf16[2,1024,128]{2,1,0:T(8,128)(2,1)} %green.1), custom_call_target="tpu_custom_call" | custom-call | tf_op jit(solution)/shard_map/pallas_call | solution.py:325
  55.6 0.6 %copy.8 = f32[2,128,32]{1,2,0:T(8,128)} copy(f32[2,128,32]{1,2,0:T(8,128)S(1)} %bitcast.5) | data formatting | bytes 65536
